TPU v7x, 256 devices: a whole 4x4x8 slice. The times are simulated.
256 devices in a mesh: band: 64 (over x, z, core), lev: 4 (over y).
Axes of the slice: x: 4, y: 4, z: 8, core: 2. Of those that a mesh axis runs over, the one named last changes fastest.
Arguments:
- obs_vals: bfloat16 [4, 24, 262144], P('lev', None, 'band'), may hold values from -400 to 400
- obs_colat: bfloat16 [262144], P('band'), may hold values from -1 to 1
- obs_lon: int32 [262144], P('band'), may hold values from 0 to 2047
- band_list: int32 [64, 64, 128], P('band'), may hold values from 0 to 4095, as said below
- counts: int32 [64, 64], P('band'), may hold values from 0 to 128, as said below
- w_in: bfloat16 [96, 256], replicated, may hold values from -0.625 to 0.625
- b_in: float32 [256], replicated, may hold values from -3 to 3
- w_out: bfloat16 [256, 256], P(None, 'lev'), may hold values from -0.375 to 0.375
- b_out: float32 [256], P('lev'), may hold values from -3 to 3
Outputs:
- encoded: bfloat16 [256, 2048, 512], P('lev', 'band')
Inputs may be any that keep to these rules, and one draw needn't show every extreme that they name: For each device s and band b the first counts[s, b] entries of band_list[s, b] are indices (within device s) of observations in band b; over all b they name every observation of device s exactly once. Later entries are padding and name arbitrary observations. `counts`: each row sums to 4096. Some band receives 128 observations from every device.
All inputs are finite; a program needn't handle non-finite values.
Results may differ from a plain program's by a relative error of at most 0.0063.
Values may be sent and summed in bfloat16 or wider, within the bound.
A program may use at most 64 MiB of HBM per device.

v0:
```python
import math
import jax
import jax.numpy as jnp
from jax import lax
from jax.sharding import PartitionSpec as P

LAT_DEV = 8
LON_DEV = 32
norm_eps = 1e-05


def cheb_inverse(nodes):
    order_ids = jnp.arange(nodes, dtype=jnp.float32)[:, None]
    node_ids = jnp.arange(nodes, dtype=jnp.float32)[None, :]
    factor = jnp.where(order_ids == 0.0, 1.0, 2.0).astype(jnp.float32) / nodes
    return factor * jnp.cos(math.pi * order_ids * (node_ids + 0.5) / nodes)


def lat_weights(colat, nodes):
    angles = jnp.arccos(jnp.clip(colat, -1.0, 1.0))
    order_ids = jnp.arange(nodes, dtype=jnp.float32)
    cheb_terms = jnp.cos(order_ids[:, None] * angles[None, :])
    return jnp.dot(cheb_inverse(nodes).T, cheb_terms, precision=lax.Precision.HIGHEST)


def dct_table(length):
    mode_ids = jnp.arange(length, dtype=jnp.float32)[:, None]
    node_ids = jnp.arange(length, dtype=jnp.float32)[None, :]
    row_scale = jnp.where(mode_ids == 0.0, math.sqrt(1.0 / length), math.sqrt(2.0 / length)).astype(
        jnp.float32
    )
    return (row_scale * jnp.cos(math.pi * mode_ids * (node_ids + 0.5) / length)).astype(
        jnp.bfloat16
    )


def on_device(obs_vals, obs_colat, obs_lon, band_list, counts, w_in, b_in, w_out, b_out):
    band_count = lax.axis_size("band")
    capacity = band_list.shape[2]
    lat_nodes = LAT_DEV
    lon_local = LON_DEV
    lon_count = lon_local * band_count
    lat_total = lat_nodes * band_count
    channels = obs_vals.shape[1]
    feat_count = w_in.shape[0]
    picked = band_list[0].reshape(-1)
    live_slot = (jnp.arange(capacity, dtype=jnp.int32)[None, :] < counts[0][:, None]).reshape(-1)
    outgoing = jnp.where(
        live_slot[None, :], jnp.take(obs_vals[0], picked, axis=1), jnp.zeros((), jnp.bfloat16)
    )
    colat_out = jnp.take(obs_colat, picked)[None, :]
    lon_out = jnp.take(obs_lon, picked)[None, :]
    incoming, colat_in, lon_in = (
        lax.all_to_all(outgoing, "band", split_axis=1, concat_axis=1, tiled=True),
        lax.all_to_all(colat_out, "band", split_axis=1, concat_axis=1, tiled=True),
        lax.all_to_all(lon_out, "band", split_axis=1, concat_axis=1, tiled=True),
    )
    weights = lat_weights(colat_in[0].astype(jnp.float32), lat_nodes)
    weighted = (incoming.astype(jnp.float32)[:, None, :] * weights[None]).astype(jnp.bfloat16)
    weighted = weighted.reshape(channels * lat_nodes, -1)
    lon_ids = lon_in[0]
    row_count = weighted.shape[1]
    block_rows = math.gcd(row_count, 1024)
    columns = jnp.arange(lon_count, dtype=jnp.int32)

    def add_block(step_index, grid_sum):
        first_row = step_index * block_rows
        block_vals = lax.dynamic_slice_in_dim(weighted, first_row, block_rows, 1)
        block_lon = lax.dynamic_slice_in_dim(lon_ids, first_row, block_rows, 0)
        onehot = (block_lon[:, None] == columns[None, :]).astype(jnp.bfloat16)
        return grid_sum + jnp.dot(block_vals, onehot, preferred_element_type=jnp.float32)

    grid_sum = lax.fori_loop(
        0,
        row_count // block_rows,
        add_block,
        jnp.zeros((channels * lat_nodes, lon_count), jnp.float32),
    )
    grid_half = grid_sum.astype(jnp.bfloat16).reshape(channels, lat_nodes, lon_count)
    all_levels = lax.all_gather(grid_half, "lev", axis=0, tiled=True)
    received = lax.all_to_all(all_levels, "band", split_axis=2, concat_axis=2, tiled=True)
    items = received.shape[0]
    arranged = received.reshape(items, lat_nodes, band_count, lon_local)
    table = dct_table(lat_total).reshape(lat_total, band_count, lat_nodes)
    spectrum = jnp.einsum(
        "cjbm,kbj->cmk", arranged, table, preferred_element_type=jnp.float32
    ).astype(jnp.bfloat16)
    pre_act = jnp.einsum("fh,fmk->hmk", w_in, spectrum, preferred_element_type=jnp.float32)
    squared = spectrum.astype(jnp.float32)
    pre_act, sum_sq = (pre_act, jnp.sum(squared * squared, axis=0))
    inv_norm = lax.rsqrt(sum_sq * (1.0 / feat_count) + norm_eps)
    hidden = jax.nn.gelu(pre_act * inv_norm[None] + b_in[:, None, None]).astype(jnp.bfloat16)
    output = (
        jnp.einsum("ho,hmk->omk", w_out, hidden, preferred_element_type=jnp.float32)
        + b_out[:, None, None]
    )
    return output.astype(jnp.bfloat16)


def solution(mesh):
    in_specs = (
        P("lev", None, "band"),
        P("band"),
        P("band"),
        P("band", None, None),
        P("band", None),
        P(),
        P(),
        P(None, "lev"),
        P("lev"),
    )
    out_specs = P("lev", "band", None)
    return jax.shard_map(
        on_device, mesh=mesh, in_specs=in_specs, out_specs=out_specs, check_vma=False
    )
```

profile of v0, /device:TPU:1, one launch (start us, length us, event | category | flops | bytes accessed | tf_op | source)
XLA Modules:
  0.0 420.4 jit_solution(8596966610472597191)
XLA Ops:
  7.4 45.5 %gather_fusion.2 = s32[8192]{0:T(1024)S(1)} fusion(s32[4096]{0:T(1024)S(1)} %copy-done.1, s32[8192]{0:T(1024)S(1)} %broadcast_clamp_fusion), kind=kCustom, calls=%fused_computation.2 | custom fusion | bytes 98304 | tf_op jit(solution)/shard_map/jit(_take)/gather | solution.py:52
  53.6 50.7 %gather_fusion.1 = bf16[8192]{0:T(1024)(128)(2,1)S(1)} fusion(bf16[4096]{0:T(1024)(128)(2,1)S(1)} %copy-done.2, s32[8192]{0:T(1024)S(1)} %broadcast_clamp_fusion), kind=kCustom, calls=%fused_computation.1 | custom fusion | bytes 65536 | tf_op jit(solution)/shard_map/jit(_take)/gather | solution.py:51
  105.0 13.0 %all-to-all-start.1 = ((bf16[1,64,128]{2,0,1:T(2,128)(2,1)}), bf16[1,64,128]{2,0,1:T(2,128)(2,1)S(1)}, u32[]{:S(2)}, u32[]{:S(2)}) async-start(bf16[1,64,128]{2,0,1:T(2,128)(2,1)} %copy.55), calls=%async_computation.1 | async-start | bytes 65536 | tf_op jit(solution)/shard_map/all_to_all | solution.py:55
  118.5 24.0 %gather_fusion = bf16[8192,24]{1,0:T(8,128)(2,1)S(1)} fusion(bf16[24,4096]{0,1:T(8,128)(2,1)S(1)} %bitcast.52, s32[8192]{0:T(1024)S(1)} %broadcast_clamp_fusion), kind=kCustom, calls=%fused_computation | custom fusion | bytes 819200 | tf_op jit(solution)/shard_map/jit(_take)/gather | solution.py:49
  144.4 10.3 %all-to-all-start = ((bf16[24,64,128]{2,0,1:T(8,128)(2,1)}), bf16[24,64,128]{2,0,1:T(8,128)(2,1)S(1)}, u32[]{:S(2)}, u32[]{:S(2)}) async-start(bf16[24,64,128]{2,0,1:T(8,128)(2,1)} %select_select_fusion), calls=%async_computation | async-start | bytes 786432 | tf_op jit(solution)/shard_map/all_to_all | solution.py:54
  156.1 13.2 %all-to-all-done = bf16[24,64,128]{2,0,1:T(8,128)(2,1)S(1)} async-done(((bf16[24,64,128]{2,0,1:T(8,128)(2,1)}), bf16[24,64,128]{2,0,1:T(8,128)(2,1)S(1)}, u32[]{:S(2)}, u32[]{:S(2)}) %all-to-all-start) | async-done | bytes 393248 | tf_op jit(solution)/shard_map/all_to_all | solution.py:54
  169.3 6.2 %all-to-all-start.2 = ((s32[1,64,128]{2,0,1:T(1,128)}), s32[1,64,128]{2,0,1:T(1,128)S(1)}, u32[]{:S(2)}, u32[]{:S(2)}) async-start(s32[1,64,128]{2,0,1:T(1,128)} %bitcast.11), calls=%async_computation.2 | async-start | bytes 65536 | tf_op jit(solution)/shard_map/all_to_all | solution.py:56
  176.1 8.7 %all-to-all-done.2 = s32[1,64,128]{2,0,1:T(1,128)S(1)} async-done(((s32[1,64,128]{2,0,1:T(1,128)}), s32[1,64,128]{2,0,1:T(1,128)S(1)}, u32[]{:S(2)}, u32[]{:S(2)}) %all-to-all-start.2) | async-done | bytes 32800 | tf_op jit(solution)/shard_map/all_to_all | solution.py:56
  184.9 35.6 %while.14 = (s32[]{:T(128)}, f32[192,2048]{1,0:T(8,128)}, bf16[192,8192]{1,0:T(8,128)(2,1)S(1)}, s32[8192]{0:T(1024)S(1)}, s32[]{:T(128)}, /*index=5*/s32[]{:T(128)}, s32[]{:T(128)}, s32[]{:T(128)}) while((s32[]{:T(128)}, f32[192,2048]{1,0:T(8,128)}, bf16[192,8192]{1,0:T(8,128)(2,1)S(1)}, s32[8192]{0:T(1024)S(1)}, s32[]{:T(128)}, ...), condition=%wide.region_1.2_spmd.clone, body=%wide.region_0.1_spmd.clone.sunk | while | flops 808189952 | bytes 3551381 | solution.py:73
  184.9 3.2 fusion.57
  188.1 4.6 %fusion.57 = f32[192,2048]{1,0:T(8,128)} fusion(s32[1024]{0:T(1024)S(1)} %dynamic_slice.21, f32[192,2048]{1,0:T(8,128)} %get-tuple-element.167, pred[]{:T(512)S(6)} %compare.3, bf16[192,8192]{1,0:T(8,128)(2,1)S(1)} %get-tuple-element.176, s32[]{:T(128)S(6)} %select_n.102), kind=kOutput, calls=%fused_computation.7.clone.1 | convolution fusion | flops 808189952 | bytes 3543045 | tf_op jit(solution)/shard_map/while/body/eval_jaxpr/dot_general | solution.py:71
  192.7 4.6 %fusion.57 = f32[192,2048]{1,0:T(8,128)} fusion(s32[1024]{0:T(1024)S(1)} %dynamic_slice.21, f32[192,2048]{1,0:T(8,128)} %get-tuple-element.167, pred[]{:T(512)S(6)} %compare.3, bf16[192,8192]{1,0:T(8,128)(2,1)S(1)} %get-tuple-element.176, s32[]{:T(128)S(6)} %select_n.102), kind=kOutput, calls=%fused_computation.7.clone.1 | convolution fusion | flops 808189952 | bytes 3543045 | tf_op jit(solution)/shard_map/while/body/eval_jaxpr/dot_general | solution.py:71
  197.3 4.6 %fusion.57 = f32[192,2048]{1,0:T(8,128)} fusion(s32[1024]{0:T(1024)S(1)} %dynamic_slice.21, f32[192,2048]{1,0:T(8,128)} %get-tuple-element.167, pred[]{:T(512)S(6)} %compare.3, bf16[192,8192]{1,0:T(8,128)(2,1)S(1)} %get-tuple-element.176, s32[]{:T(128)S(6)} %select_n.102), kind=kOutput, calls=%fused_computation.7.clone.1 | convolution fusion | flops 808189952 | bytes 3543045 | tf_op jit(solution)/shard_map/while/body/eval_jaxpr/dot_general | solution.py:71
  202.0 4.6 %fusion.57 = f32[192,2048]{1,0:T(8,128)} fusion(s32[1024]{0:T(1024)S(1)} %dynamic_slice.21, f32[192,2048]{1,0:T(8,128)} %get-tuple-element.167, pred[]{:T(512)S(6)} %compare.3, bf16[192,8192]{1,0:T(8,128)(2,1)S(1)} %get-tuple-element.176, s32[]{:T(128)S(6)} %select_n.102), kind=kOutput, calls=%fused_computation.7.clone.1 | convolution fusion | flops 808189952 | bytes 3543045 | tf_op jit(solution)/shard_map/while/body/eval_jaxpr/dot_general | solution.py:71
  206.6 4.6 %fusion.57 = f32[192,2048]{1,0:T(8,128)} fusion(s32[1024]{0:T(1024)S(1)} %dynamic_slice.21, f32[192,2048]{1,0:T(8,128)} %get-tuple-element.167, pred[]{:T(512)S(6)} %compare.3, bf16[192,8192]{1,0:T(8,128)(2,1)S(1)} %get-tuple-element.176, s32[]{:T(128)S(6)} %select_n.102), kind=kOutput, calls=%fused_computation.7.clone.1 | convolution fusion | flops 808189952 | bytes 3543045 | tf_op jit(solution)/shard_map/while/body/eval_jaxpr/dot_general | solution.py:71
  211.2 4.6 %fusion.57 = f32[192,2048]{1,0:T(8,128)} fusion(s32[1024]{0:T(1024)S(1)} %dynamic_slice.21, f32[192,2048]{1,0:T(8,128)} %get-tuple-element.167, pred[]{:T(512)S(6)} %compare.3, bf16[192,8192]{1,0:T(8,128)(2,1)S(1)} %get-tuple-element.176, s32[]{:T(128)S(6)} %select_n.102), kind=kOutput, calls=%fused_computation.7.clone.1 | convolution fusion | flops 808189952 | bytes 3543045 | tf_op jit(solution)/shard_map/while/body/eval_jaxpr/dot_general | solution.py:71
  215.9 4.6 %fusion.57 = f32[192,2048]{1,0:T(8,128)} fusion(s32[1024]{0:T(1024)S(1)} %dynamic_slice.21, f32[192,2048]{1,0:T(8,128)} %get-tuple-element.167, pred[]{:T(512)S(6)} %compare.3, bf16[192,8192]{1,0:T(8,128)(2,1)S(1)} %get-tuple-element.176, s32[]{:T(128)S(6)} %select_n.102), kind=kOutput, calls=%fused_computation.7.clone.1 | convolution fusion | flops 808189952 | bytes 3543045 | tf_op jit(solution)/shard_map/while/body/eval_jaxpr/dot_general | solution.py:71
  222.9 36.9 %all-gather.2.cloned.1.call-done = bf16[96,8,2048]{2,1,0:T(8,128)(2,1)} async-done(((bf16[24,8,2048]{2,1,0:T(8,128)(2,1)}), bf16[96,8,2048]{2,1,0:T(8,128)(2,1)}) %all-gather.2.cloned.1.call-update) | async-done | bytes 3145744 | tf_op jit(solution)/shard_map/all_gather | solution.py:80
  259.9 7.0 %copy.57 = bf16[96,8,2048]{0,1,2:T(8,128)(2,1)} copy(bf16[96,8,2048]{2,1,0:T(8,128)(2,1)} %all-gather.2.cloned.1.call-done) | data formatting | bytes 6291456 | tf_op jit(solution)/shard_map/all_gather | solution.py:80
  266.9 11.0 %all-to-all-start.3 = ((bf16[96,8,2048]{0,1,2:T(8,128)(2,1)}), bf16[96,8,2048]{0,1,2:T(8,128)(2,1)}, u32[]{:S(2)}, u32[]{:S(2)}) async-start(bf16[96,8,2048]{0,1,2:T(8,128)(2,1)} %copy.57), calls=%async_computation.3 | async-start | bytes 8388608 | tf_op jit(solution)/shard_map/all_to_all | solution.py:81
  277.9 95.8 %all-to-all-done.3 = bf16[96,8,2048]{0,1,2:T(8,128)(2,1)} async-done(((bf16[96,8,2048]{0,1,2:T(8,128)(2,1)}), bf16[96,8,2048]{0,1,2:T(8,128)(2,1)}, u32[]{:S(2)}, u32[]{:S(2)}) %all-to-all-start.3) | async-done | bytes 3145760 | tf_op jit(solution)/shard_map/all_to_all | solution.py:81
  373.7 13.4 %copy.59 = bf16[96,8,64,32]{2,3,1,0:T(8,128)(2,1)} copy(bf16[96,8,64,32]{0,1,3,2:T(8,128)(2,1)} %bitcast.14) | data formatting | bytes 6291456 | tf_op jit(solution)/shard_map/reshape | solution.py:83
  387.1 11.2 %multiply_reduce_fusion = (f32[32,512]{1,0:T(8,128)S(1)}, bf16[96,32,512]{2,1,0:T(8,128)(2,1)}) fusion(bf16[96,8,64,32]{2,3,1,0:T(8,128)(2,1)} %copy.59, f32[64,8]{0,1:T(8,128)S(1)} %add_add_fusion, f32[512]{0:T(512)S(1)} %get-tuple-element.131, f32[512]{0:T(512)S(1)} %get-tuple-element.132), kind=kOutput, calls=%fused_computation.20 | convolution fusion | flops 1617936384 | bytes 6363136 | tf_op jit(solution)/shard_map/cjbm,kbj->cmk/dot_general | solution.py:85
  398.3 12.7 %fusion.20 = bf16[64,32,512]{2,0,1:T(8,128)(2,1)S(1)} fusion(f32[64]{0:T(128)S(1)} %copy-done.8, f32[256]{0:T(256)S(1)} %copy-done.7, f32[32,512]{1,0:T(8,128)S(1)} %add_rsqrt_fusion, bf16[96,32,512]{2,1,0:T(8,128)(2,1)} %get-tuple-element.128, bf16[96,256]{1,0:T(8,128)(2,1)S(1)} %copy-done, bf16[256,64]{0,1:T(8,128)(2,1)S(1)} %copy-done.6), kind=kOutput, calls=%fused_computation.26 | convolution fusion | flops 1390411776 | bytes 5391616 | tf_op jit(solution)/shard_map/ho,hmk->omk/dot_general | solution.py:94
  (52 shorter events, 11.4 us)
Async XLA Ops:
  6.5 391.7 %copy-start = (bf16[96,256]{1,0:T(8,128)(2,1)S(1)}, bf16[96,256]{1,0:T(8,128)(2,1)}, u32[]{:S(2)}) copy-start(bf16[96,256]{1,0:T(8,128)(2,1)} %param.16) | copy-start | bytes 147460
  6.5 0.8 copy-start.1
  7.4 45.6 %copy-start.3 = (s32[1,64,128]{2,1,0:T(8,128)S(1)}, s32[1,64,128]{2,1,0:T(8,128)}, u32[]{:S(2)}) copy-start(s32[1,64,128]{2,1,0:T(8,128)} %param.14) | copy-start | bytes 98308
  52.9 0.7 copy-start.2
  53.6 64.4 %copy-start.4 = (bf16[1,24,4096]{2,1,0:T(8,128)(2,1)S(1)}, bf16[1,24,4096]{2,1,0:T(8,128)(2,1)}, u32[]{:S(2)}) copy-start(bf16[1,24,4096]{2,1,0:T(8,128)(2,1)} %param.11) | copy-start | bytes 589828
  104.4 39.1 %copy-start.5 = (s32[1,64]{1,0:T(1,128)S(1)}, s32[1,64]{1,0:T(1,128)}, u32[]{:S(2)}) copy-start(s32[1,64]{1,0:T(1,128)} %param.15) | copy-start | bytes 772
  105.0 39.4 %all-to-all-start.1 = ((bf16[1,64,128]{2,0,1:T(2,128)(2,1)}), bf16[1,64,128]{2,0,1:T(2,128)(2,1)S(1)}, u32[]{:S(2)}, u32[]{:S(2)}) async-start(bf16[1,64,128]{2,0,1:T(2,128)(2,1)} %copy.55), calls=%async_computation.1 | async-start | bytes 65536 | tf_op jit(solution)/shard_map/all_to_all | solution.py:55
  144.4 24.9 %all-to-all-start = ((bf16[24,64,128]{2,0,1:T(8,128)(2,1)}), bf16[24,64,128]{2,0,1:T(8,128)(2,1)S(1)}, u32[]{:S(2)}, u32[]{:S(2)}) async-start(bf16[24,64,128]{2,0,1:T(8,128)(2,1)} %select_select_fusion), calls=%async_computation | async-start | bytes 786432 | tf_op jit(solution)/shard_map/all_to_all | solution.py:54
  169.3 15.6 %all-to-all-start.2 = ((s32[1,64,128]{2,0,1:T(1,128)}), s32[1,64,128]{2,0,1:T(1,128)S(1)}, u32[]{:S(2)}, u32[]{:S(2)}) async-start(s32[1,64,128]{2,0,1:T(1,128)} %bitcast.11), calls=%async_computation.2 | async-start | bytes 65536 | tf_op jit(solution)/shard_map/all_to_all | solution.py:56
  175.5 84.3 %all-gather.2.cloned.1.call-start = ((), (), s32[]{:S(2)}) async-start(), calls=%async_computation.4 | async-start | bytes 3932160 | tf_op jit(solution)/shard_map/all_gather | solution.py:80
  266.9 106.9 %all-to-all-start.3 = ((bf16[96,8,2048]{0,1,2:T(8,128)(2,1)}), bf16[96,8,2048]{0,1,2:T(8,128)(2,1)}, u32[]{:S(2)}, u32[]{:S(2)}) async-start(bf16[96,8,2048]{0,1,2:T(8,128)(2,1)} %copy.57), calls=%async_computation.3 | async-start | bytes 8388608 | tf_op jit(solution)/shard_map/all_to_all | solution.py:81
  387.1 11.2 %copy-start.6 = (bf16[256,64]{0,1:T(8,128)(2,1)S(1)}, bf16[256,64]{0,1:T(8,128)(2,1)}, u32[]{:S(2)}) copy-start(bf16[256,64]{0,1:T(8,128)(2,1)} %param.18) | copy-start | bytes 98308
  387.1 11.2 %copy-start.7 = (f32[256]{0:T(256)S(1)}, f32[256]{0:T(256)}, u32[]{:S(2)}) copy-start(f32[256]{0:T(256)} %param.17) | copy-start | bytes 3076
  387.1 11.2 %copy-start.8 = (f32[64]{0:T(128)S(1)}, f32[64]{0:T(128)}, u32[]{:S(2)}) copy-start(f32[64]{0:T(128)} %param.19) | copy-start | bytes 772
Sparse Core Ops, SparseCore 0:
  223.1 36.7 all-gather.1
where the time goes:
time: 421 us; the launch traced here: 420 us
  waiting for transfers between devices  155 us (37%)
  local copies, waits for them, and re-layouts  145 us (34%)
  matrix products  60.7 us (14%)
  starting transfers between devices  40.6 us (10%)
  between operations  13.7 us (3%)
  other arithmetic  5.5 us (1%)
    all_to_all x1, waiting for transfers between devices, on_device(): lax.all_to_all(all_levels, 'band', split_axis=2, concat_axis=2, tiled=True)  95.8 us
    gather x1, local copies, waits for them, and re-layouts, on_device(): colat_out = jnp.take(obs_colat, picked)[None, :]  50.7 us
    gather x1, local copies, waits for them, and re-layouts, on_device(): lon_out = jnp.take(obs_lon, picked)[None, :]  45.5 us
    all_gather x1, waiting for transfers between devices, on_device(): all_levels = lax.all_gather(grid_half, 'lev', axis=0, tiled=True)  36.9 us
    dot_general x8, matrix products, add_block(): jnp.dot(block_vals, onehot, preferred_element_type=jnp.float32)  35.6 us
    gather x2, local copies, waits for them, and re-layouts, on_device(): jnp.take(obs_vals[0], picked, axis=1)  24.9 us
    reshape x1, local copies, waits for them, and re-layouts, on_device(): arranged = received.reshape(items, lat_nodes, band_count, lon_local)  13.4 us
    all_to_all x1, waiting for transfers between devices, on_device(): lax.all_to_all(outgoing, 'band', split_axis=1, concat_axis=1, tiled=True)  13.2 us
  transfers between devices with their start and end apart: 5, of which 4 were waited for; matrix products, arithmetic and copies ran while one was open for 7% of the time, Pallas kernels for 0%

commit v1 on v0

--- a/solution.py
+++ b/solution.py
@@ -77,7 +77,9 @@
         jnp.zeros((channels * lat_nodes, lon_count), jnp.float32),
     )
     grid_half = grid_sum.astype(jnp.bfloat16).reshape(channels, lat_nodes, lon_count)
-    all_levels = lax.all_gather(grid_half, "lev", axis=0, tiled=True)
+    all_levels = jnp.concatenate(
+        lax.all_to_all(jnp.stack([grid_half] * lax.axis_size("lev")), "lev", 0, 0), axis=0
+    )
     received = lax.all_to_all(all_levels, "band", split_axis=2, concat_axis=2, tiled=True)
     items = received.shape[0]
     arranged = received.reshape(items, lat_nodes, band_count, lon_local)

time: 421 us -> 405 us (0.962)
  blocking collectives: 0 us -> 40.7 us
  waiting for transfers between devices: 155 us -> 118 us
  between operations: 13.7 us -> 0.27 us
    all_to_all x0 -> x1, blocking collectives: none -> 40.7 us  [on_device(): lax.all_to_all(jnp.stack([grid_half] * lax.axis_size('lev')), 'lev', 0, 0)]
    all_gather x1 -> x0, waiting for transfers between devices: 36.9 us -> none  [on_device(): all_levels = lax.all_gather(grid_half, 'lev', axis=0, tiled=True)]
    all_gather x1 -> x0, local copies, waits for them, and re-layouts: 7.01 us -> none  [on_device(): all_levels = lax.all_gather(grid_half, 'lev', axis=0, tiled=True)]
    reshape x0 -> x1, local copies, waits for them, and re-layouts: none -> 5.19 us  [on_device(): jnp.concatenate(lax.all_to_all(jnp.stack([grid_half] * lax.axis_size('lev...]
  transfers between devices with their start and end apart: 5 -> 4, of which waited for: 4 -> 3; matrix products, arithmetic and copies ran while one was open for 7% -> 7% of each run, Pallas kernels for 0% -> 0%
where the time goes in v1:
time: 405 us; the launch traced here: 404 us
  local copies, waits for them, and re-layouts  144 us (36%)
  waiting for transfers between devices  118 us (29%)
  matrix products  60.8 us (15%)
  blocking collectives  40.7 us (10%)
  starting transfers between devices  36.4 us (9%)
  other arithmetic  4.58 us (1%)
    all_to_all x1, waiting for transfers between devices, on_device(): lax.all_to_all(all_levels, 'band', split_axis=2, concat_axis=2, tiled=True)  95.9 us
    gather x1, local copies, waits for them, and re-layouts, on_device(): colat_out = jnp.take(obs_colat, picked)[None, :]  50.7 us
    gather x1, local copies, waits for them, and re-layouts, on_device(): lon_out = jnp.take(obs_lon, picked)[None, :]  45.5 us
    all_to_all x1, blocking collectives, on_device(): lax.all_to_all(jnp.stack([grid_half] * lax.axis_size('lev')), 'lev', 0, 0)  40.7 us
    dot_general x8, matrix products, add_block(): jnp.dot(block_vals, onehot, preferred_element_type=jnp.float32)  35.6 us
    gather x2, local copies, waits for them, and re-layouts, on_device(): jnp.take(obs_vals[0], picked, axis=1)  24.9 us
    reshape x1, local copies, waits for them, and re-layouts, on_device(): arranged = received.reshape(items, lat_nodes, band_count, lon_local)  13.4 us
    all_to_all x1, waiting for transfers between devices, on_device(): lax.all_to_all(outgoing, 'band', split_axis=1, concat_axis=1, tiled=True)  13.2 us
  transfers between devices with their start and end apart: 4, of which 3 were waited for; matrix products, arithmetic and copies ran while one was open for 7% of the time, Pallas kernels for 0%

profile of v1, /device:TPU:1, one launch (start us, length us, event | category | flops | bytes accessed | tf_op | source)
XLA Modules:
  0.0 404.3 jit_solution(15577049272050844059)
XLA Ops:
  0.9 45.5 %gather_fusion.2 = s32[8192]{0:T(1024)S(1)} fusion(s32[4096]{0:T(1024)S(1)} %copy-done.1, s32[8192]{0:T(1024)S(1)} %broadcast_clamp_fusion), kind=kCustom, calls=%fused_computation.2 | custom fusion | bytes 98304 | tf_op jit(solution)/shard_map/jit(_take)/gather | solution.py:52
  47.1 50.7 %gather_fusion.1 = bf16[8192]{0:T(1024)(128)(2,1)S(1)} fusion(bf16[4096]{0:T(1024)(128)(2,1)S(1)} %copy-done.2, s32[8192]{0:T(1024)S(1)} %broadcast_clamp_fusion), kind=kCustom, calls=%fused_computation.1 | custom fusion | bytes 65536 | tf_op jit(solution)/shard_map/jit(_take)/gather | solution.py:51
  98.5 13.0 %all-to-all-start.1 = ((bf16[1,64,128]{2,0,1:T(2,128)(2,1)}), bf16[1,64,128]{2,0,1:T(2,128)(2,1)S(1)}, u32[]{:S(2)}, u32[]{:S(2)}) async-start(bf16[1,64,128]{2,0,1:T(2,128)(2,1)} %copy.56), calls=%async_computation.1 | async-start | bytes 65536 | tf_op jit(solution)/shard_map/all_to_all | solution.py:55
  112.0 24.0 %gather_fusion = bf16[8192,24]{1,0:T(8,128)(2,1)S(1)} fusion(bf16[24,4096]{0,1:T(8,128)(2,1)S(1)} %bitcast.53, s32[8192]{0:T(1024)S(1)} %broadcast_clamp_fusion), kind=kCustom, calls=%fused_computation | custom fusion | bytes 819200 | tf_op jit(solution)/shard_map/jit(_take)/gather | solution.py:49
  137.8 10.3 %all-to-all-start = ((bf16[24,64,128]{2,0,1:T(8,128)(2,1)}), bf16[24,64,128]{2,0,1:T(8,128)(2,1)S(1)}, u32[]{:S(2)}, u32[]{:S(2)}) async-start(bf16[24,64,128]{2,0,1:T(8,128)(2,1)} %select_select_fusion), calls=%async_computation | async-start | bytes 786432 | tf_op jit(solution)/shard_map/all_to_all | solution.py:54
  149.6 13.2 %all-to-all-done = bf16[24,64,128]{2,0,1:T(8,128)(2,1)S(1)} async-done(((bf16[24,64,128]{2,0,1:T(8,128)(2,1)}), bf16[24,64,128]{2,0,1:T(8,128)(2,1)S(1)}, u32[]{:S(2)}, u32[]{:S(2)}) %all-to-all-start) | async-done | bytes 393248 | tf_op jit(solution)/shard_map/all_to_all | solution.py:54
  162.7 6.2 %all-to-all-start.2 = ((s32[1,64,128]{2,0,1:T(1,128)}), s32[1,64,128]{2,0,1:T(1,128)S(1)}, u32[]{:S(2)}, u32[]{:S(2)}) async-start(s32[1,64,128]{2,0,1:T(1,128)} %bitcast.11), calls=%async_computation.2 | async-start | bytes 65536 | tf_op jit(solution)/shard_map/all_to_all | solution.py:56
  169.5 8.8 %all-to-all-done.2 = s32[1,64,128]{2,0,1:T(1,128)S(1)} async-done(((s32[1,64,128]{2,0,1:T(1,128)}), s32[1,64,128]{2,0,1:T(1,128)S(1)}, u32[]{:S(2)}, u32[]{:S(2)}) %all-to-all-start.2) | async-done | bytes 32800 | tf_op jit(solution)/shard_map/all_to_all | solution.py:56
  178.3 35.6 %while.14 = (s32[]{:T(128)}, f32[192,2048]{1,0:T(8,128)}, bf16[192,8192]{1,0:T(8,128)(2,1)S(1)}, s32[8192]{0:T(1024)S(1)}, s32[]{:T(128)}, /*index=5*/s32[]{:T(128)}, s32[]{:T(128)}, s32[]{:T(128)}) while((s32[]{:T(128)}, f32[192,2048]{1,0:T(8,128)}, bf16[192,8192]{1,0:T(8,128)(2,1)S(1)}, s32[8192]{0:T(1024)S(1)}, s32[]{:T(128)}, ...), condition=%wide.region_1.2_spmd.clone, body=%wide.region_0.1_spmd.clone.sunk | while | flops 808189952 | bytes 3551381 | solution.py:73
  178.3 3.2 fusion.57
  181.5 4.6 %fusion.57 = f32[192,2048]{1,0:T(8,128)} fusion(s32[1024]{0:T(1024)S(1)} %dynamic_slice.21, f32[192,2048]{1,0:T(8,128)} %get-tuple-element.167, pred[]{:T(512)S(6)} %compare.3, bf16[192,8192]{1,0:T(8,128)(2,1)S(1)} %get-tuple-element.176, s32[]{:T(128)S(6)} %select_n.102), kind=kOutput, calls=%fused_computation.7.clone.1 | convolution fusion | flops 808189952 | bytes 3543045 | tf_op jit(solution)/shard_map/while/body/eval_jaxpr/dot_general | solution.py:71
  186.2 4.6 %fusion.57 = f32[192,2048]{1,0:T(8,128)} fusion(s32[1024]{0:T(1024)S(1)} %dynamic_slice.21, f32[192,2048]{1,0:T(8,128)} %get-tuple-element.167, pred[]{:T(512)S(6)} %compare.3, bf16[192,8192]{1,0:T(8,128)(2,1)S(1)} %get-tuple-element.176, s32[]{:T(128)S(6)} %select_n.102), kind=kOutput, calls=%fused_computation.7.clone.1 | convolution fusion | flops 808189952 | bytes 3543045 | tf_op jit(solution)/shard_map/while/body/eval_jaxpr/dot_general | solution.py:71
  190.8 4.6 %fusion.57 = f32[192,2048]{1,0:T(8,128)} fusion(s32[1024]{0:T(1024)S(1)} %dynamic_slice.21, f32[192,2048]{1,0:T(8,128)} %get-tuple-element.167, pred[]{:T(512)S(6)} %compare.3, bf16[192,8192]{1,0:T(8,128)(2,1)S(1)} %get-tuple-element.176, s32[]{:T(128)S(6)} %select_n.102), kind=kOutput, calls=%fused_computation.7.clone.1 | convolution fusion | flops 808189952 | bytes 3543045 | tf_op jit(solution)/shard_map/while/body/eval_jaxpr/dot_general | solution.py:71
  195.4 4.6 %fusion.57 = f32[192,2048]{1,0:T(8,128)} fusion(s32[1024]{0:T(1024)S(1)} %dynamic_slice.21, f32[192,2048]{1,0:T(8,128)} %get-tuple-element.167, pred[]{:T(512)S(6)} %compare.3, bf16[192,8192]{1,0:T(8,128)(2,1)S(1)} %get-tuple-element.176, s32[]{:T(128)S(6)} %select_n.102), kind=kOutput, calls=%fused_computation.7.clone.1 | convolution fusion | flops 808189952 | bytes 3543045 | tf_op jit(solution)/shard_map/while/body/eval_jaxpr/dot_general | solution.py:71
  200.1 4.6 %fusion.57 = f32[192,2048]{1,0:T(8,128)} fusion(s32[1024]{0:T(1024)S(1)} %dynamic_slice.21, f32[192,2048]{1,0:T(8,128)} %get-tuple-element.167, pred[]{:T(512)S(6)} %compare.3, bf16[192,8192]{1,0:T(8,128)(2,1)S(1)} %get-tuple-element.176, s32[]{:T(128)S(6)} %select_n.102), kind=kOutput, calls=%fused_computation.7.clone.1 | convolution fusion | flops 808189952 | bytes 3543045 | tf_op jit(solution)/shard_map/while/body/eval_jaxpr/dot_general | solution.py:71
  204.7 4.6 %fusion.57 = f32[192,2048]{1,0:T(8,128)} fusion(s32[1024]{0:T(1024)S(1)} %dynamic_slice.21, f32[192,2048]{1,0:T(8,128)} %get-tuple-element.167, pred[]{:T(512)S(6)} %compare.3, bf16[192,8192]{1,0:T(8,128)(2,1)S(1)} %get-tuple-element.176, s32[]{:T(128)S(6)} %select_n.102), kind=kOutput, calls=%fused_computation.7.clone.1 | convolution fusion | flops 808189952 | bytes 3543045 | tf_op jit(solution)/shard_map/while/body/eval_jaxpr/dot_general | solution.py:71
  209.3 4.6 %fusion.57 = f32[192,2048]{1,0:T(8,128)} fusion(s32[1024]{0:T(1024)S(1)} %dynamic_slice.21, f32[192,2048]{1,0:T(8,128)} %get-tuple-element.167, pred[]{:T(512)S(6)} %compare.3, bf16[192,8192]{1,0:T(8,128)(2,1)S(1)} %get-tuple-element.176, s32[]{:T(128)S(6)} %select_n.102), kind=kOutput, calls=%fused_computation.7.clone.1 | convolution fusion | flops 808189952 | bytes 3543045 | tf_op jit(solution)/shard_map/while/body/eval_jaxpr/dot_general | solution.py:71
  215.9 40.7 %all_to_all.28 = bf16[4,24,8,2048]{3,2,1,0:T(8,128)(2,1)S(1)} all-to-all(bf16[4,24,8,2048]{3,2,1,0:T(8,128)(2,1)S(1)} %stack.3), channel_id=1, replica_groups=mesh['band'=64,'lev'=4] {'lev'}, dimensions={0} | all-to-all | bytes 6291456 | tf_op jit(solution)/shard_map/all_to_all | solution.py:81
  256.5 5.2 %copy.58 = bf16[96,8,2048]{0,1,2:T(8,128)(2,1)} copy(bf16[96,8,2048]{2,1,0:T(8,128)(2,1)S(1)} %bitcast.54) | data formatting | bytes 6291456 | tf_op jit(solution)/shard_map/reshape | solution.py:80
  261.7 6.8 %all-to-all-start.4 = ((bf16[96,8,2048]{0,1,2:T(8,128)(2,1)}), bf16[96,8,2048]{0,1,2:T(8,128)(2,1)}, u32[]{:S(2)}, u32[]{:S(2)}) async-start(bf16[96,8,2048]{0,1,2:T(8,128)(2,1)} %copy.58), calls=%async_computation.4 | async-start | bytes 8388608 | tf_op jit(solution)/shard_map/all_to_all | solution.py:83
  268.6 95.9 %all-to-all-done.4 = bf16[96,8,2048]{0,1,2:T(8,128)(2,1)} async-done(((bf16[96,8,2048]{0,1,2:T(8,128)(2,1)}), bf16[96,8,2048]{0,1,2:T(8,128)(2,1)}, u32[]{:S(2)}, u32[]{:S(2)}) %all-to-all-start.4) | async-done | bytes 3145760 | tf_op jit(solution)/shard_map/all_to_all | solution.py:83
  364.5 13.4 %copy.60 = bf16[96,8,64,32]{2,3,1,0:T(8,128)(2,1)} copy(bf16[96,8,64,32]{0,1,3,2:T(8,128)(2,1)} %bitcast.15) | data formatting | bytes 6291456 | tf_op jit(solution)/shard_map/reshape | solution.py:85
  377.8 11.2 %multiply_reduce_fusion = (f32[32,512]{1,0:T(8,128)S(1)}, bf16[96,32,512]{2,1,0:T(8,128)(2,1)}) fusion(bf16[96,8,64,32]{2,3,1,0:T(8,128)(2,1)} %copy.60, f32[64,8]{0,1:T(8,128)S(1)} %add_add_fusion, f32[512]{0:T(512)S(1)} %get-tuple-element.131, f32[512]{0:T(512)S(1)} %get-tuple-element.132), kind=kOutput, calls=%fused_computation.20 | convolution fusion | flops 1617936384 | bytes 6363136 | tf_op jit(solution)/shard_map/cjbm,kbj->cmk/dot_general | solution.py:87
  389.1 12.7 %fusion.20 = bf16[64,32,512]{2,0,1:T(8,128)(2,1)S(1)} fusion(f32[64]{0:T(128)S(1)} %copy-done.8, f32[256]{0:T(256)S(1)} %copy-done.7, f32[32,512]{1,0:T(8,128)S(1)} %add_rsqrt_fusion, bf16[96,32,512]{2,1,0:T(8,128)(2,1)} %get-tuple-element.128, bf16[96,256]{1,0:T(8,128)(2,1)S(1)} %copy-done, bf16[256,64]{0,1:T(8,128)(2,1)S(1)} %copy-done.6), kind=kOutput, calls=%fused_computation.26 | convolution fusion | flops 1390411776 | bytes 5391616 | tf_op jit(solution)/shard_map/ho,hmk->omk/dot_general | solution.py:96
  (51 shorter events, 10.8 us)
Async XLA Ops:
  0.0 389.0 %copy-start = (bf16[96,256]{1,0:T(8,128)(2,1)S(1)}, bf16[96,256]{1,0:T(8,128)(2,1)}, u32[]{:S(2)}) copy-start(bf16[96,256]{1,0:T(8,128)(2,1)} %param.16) | copy-start | bytes 147460
  0.0 0.8 copy-start.1
  0.8 45.6 %copy-start.3 = (s32[1,64,128]{2,1,0:T(8,128)S(1)}, s32[1,64,128]{2,1,0:T(8,128)}, u32[]{:S(2)}) copy-start(s32[1,64,128]{2,1,0:T(8,128)} %param.14) | copy-start | bytes 98308
  46.4 0.7 copy-start.2
  47.1 64.4 %copy-start.4 = (bf16[1,24,4096]{2,1,0:T(8,128)(2,1)S(1)}, bf16[1,24,4096]{2,1,0:T(8,128)(2,1)}, u32[]{:S(2)}) copy-start(bf16[1,24,4096]{2,1,0:T(8,128)(2,1)} %param.11) | copy-start | bytes 589828
  97.8 39.0 %copy-start.5 = (s32[1,64]{1,0:T(1,128)S(1)}, s32[1,64]{1,0:T(1,128)}, u32[]{:S(2)}) copy-start(s32[1,64]{1,0:T(1,128)} %param.15) | copy-start | bytes 772
  98.5 39.4 %all-to-all-start.1 = ((bf16[1,64,128]{2,0,1:T(2,128)(2,1)}), bf16[1,64,128]{2,0,1:T(2,128)(2,1)S(1)}, u32[]{:S(2)}, u32[]{:S(2)}) async-start(bf16[1,64,128]{2,0,1:T(2,128)(2,1)} %copy.56), calls=%async_computation.1 | async-start | bytes 65536 | tf_op jit(solution)/shard_map/all_to_all | solution.py:55
  137.8 24.9 %all-to-all-start = ((bf16[24,64,128]{2,0,1:T(8,128)(2,1)}), bf16[24,64,128]{2,0,1:T(8,128)(2,1)S(1)}, u32[]{:S(2)}, u32[]{:S(2)}) async-start(bf16[24,64,128]{2,0,1:T(8,128)(2,1)} %select_select_fusion), calls=%async_computation | async-start | bytes 786432 | tf_op jit(solution)/shard_map/all_to_all | solution.py:54
  162.7 15.6 %all-to-all-start.2 = ((s32[1,64,128]{2,0,1:T(1,128)}), s32[1,64,128]{2,0,1:T(1,128)S(1)}, u32[]{:S(2)}, u32[]{:S(2)}) async-start(s32[1,64,128]{2,0,1:T(1,128)} %bitcast.11), calls=%async_computation.2 | async-start | bytes 65536 | tf_op jit(solution)/shard_map/all_to_all | solution.py:56
  261.7 102.7 %all-to-all-start.4 = ((bf16[96,8,2048]{0,1,2:T(8,128)(2,1)}), bf16[96,8,2048]{0,1,2:T(8,128)(2,1)}, u32[]{:S(2)}, u32[]{:S(2)}) async-start(bf16[96,8,2048]{0,1,2:T(8,128)(2,1)} %copy.58), calls=%async_computation.4 | async-start | bytes 8388608 | tf_op jit(solution)/shard_map/all_to_all | solution.py:83
  377.8 11.2 %copy-start.6 = (bf16[256,64]{0,1:T(8,128)(2,1)S(1)}, bf16[256,64]{0,1:T(8,128)(2,1)}, u32[]{:S(2)}) copy-start(bf16[256,64]{0,1:T(8,128)(2,1)} %param.18) | copy-start | bytes 98308
  377.8 11.2 %copy-start.7 = (f32[256]{0:T(256)S(1)}, f32[256]{0:T(256)}, u32[]{:S(2)}) copy-start(f32[256]{0:T(256)} %param.17) | copy-start | bytes 3076
  377.8 11.2 %copy-start.8 = (f32[64]{0:T(128)S(1)}, f32[64]{0:T(128)}, u32[]{:S(2)}) copy-start(f32[64]{0:T(128)} %param.19) | copy-start | bytes 772
